TPU v7x, 32 devices: a whole 2x2x4 slice. The times are simulated.
32 devices in a mesh: parts: 1, rows: 8 (over z, y), branch: 2 (over core), head: 2 (over x).
Axes of the slice: x: 2, y: 2, z: 4, core: 2. Of those that a mesh axis runs over, the one named last changes fastest.
Arguments:
- lineup_state: bfloat16 [32, 128, 256], P(('parts', 'rows', 'branch')), may hold values from -12 to 12
- pairwise: bfloat16 [128, 128, 128], P(('parts', 'rows', 'branch')), may hold values from -12 to 12
- aligned_residue_bounds: int32 [32, 2], P('parts'), may hold values from 0 to 128, as said below
- residue_valid_mask: int32 [128], P('parts'), may hold values from 0 to 1, as said below
- coupling_offset_weight_map: bfloat16 [128, 8], P(None, 'head'), may hold values from -0.5 to 0.5
- triangle_bias_matrix: bfloat16 [128, 4], P(None, 'head'), may hold values from -0.5 to 0.5
- alignment_projection_matrix: bfloat16 [4, 256, 256], P(None, None, 'head'), may hold values from -1 to 1
- lineup_readout_weight: bfloat16 [256, 256], replicated, may hold values from -4 to 4
- feedfwd_entry_weight: bfloat16 [256, 1024], P(None, 'head'), may hold values from -0.375 to 0.375
- feedfwd_exit_weight: bfloat16 [1024, 256], P('head'), may hold values from -0.1875 to 0.1875
- pair_projection_matrix: bfloat16 [4, 128, 128], P(None, None, 'head'), may hold values from -2 to 2
- pair_output_matrix: bfloat16 [128, 128], P(None, 'head'), may hold values from -6 to 6
- left_right_maps: bfloat16 [2, 256, 32], replicated, may hold values from -0.375 to 0.375
- outer_product_output_matrix: bfloat16 [1024, 128], P(None, 'head'), may hold values from -1.5 to 1.5
Outputs:
- refreshed_lineup_state: bfloat16 [32, 128, 256], P(('parts', 'rows', 'branch'), None, 'head')
- pairwise_out: bfloat16 [128, 128, 128], P(('parts', 'rows', 'branch'), None, 'head')
Inputs may be any that keep to these rules, and one draw needn't show every extreme that they name: `aligned_residue_bounds`: each row holds a start below its end; row 0 covers all 128 residues; every span covers a quarter of the 128 residues or more and starts in the first half. `residue_valid_mask`: 1 on a prefix that holds at least half of the 128 residues, 0 after it; the last residue is always 0.
All inputs are finite; a program needn't handle non-finite values.
Results may differ from a plain program's by a relative error of at most 0.011.
Values may be sent and summed in bfloat16 or wider, within the bound.
No kernel may reach another device: no remote copies, remote signals or barrier semaphores. Data moves between devices by JAX's collectives and lax.ppermute only.
A program may use at most 64 MiB of HBM per device.

v0:
```python
import math
import jax
import jax.numpy as jnp
from jax import lax
from jax.sharding import PartitionSpec as P

PER_FOCUS_DIM = 32


def layer_normalize(values):
    values = values.astype(jnp.float32)
    center = values - jnp.mean(values, -1, keepdims=True)
    spread = jnp.mean(center * center, -1, keepdims=True)
    return center * lax.rsqrt(spread + 1e-05)


def soft_weights(attention_scores):
    row_max = jnp.max(attention_scores, -1, keepdims=True)
    shifted = jnp.exp(attention_scores - row_max)
    return (shifted / jnp.sum(shifted, -1, keepdims=True)).astype(jnp.bfloat16)


def span_mask(aligned_residue_bounds, length_value):
    places = jnp.arange(length_value, dtype=jnp.int32)
    inside = (places[None, :] >= aligned_residue_bounds[:, 0:1]) & (
        places[None, :] < aligned_residue_bounds[:, 1:2]
    )
    return inside.astype(jnp.float32)


def local(
    lineup_state,
    pairwise,
    aligned_residue_bounds,
    residue_valid_mask,
    coupling_offset_weight_map,
    triangle_bias_matrix,
    alignment_projection_matrix,
    lineup_readout_weight,
    feedfwd_entry_weight,
    feedfwd_exit_weight,
    pair_projection_matrix,
    pair_output_matrix,
    left_right_maps,
    outer_product_output_matrix,
):
    sequence_shard_count = lineup_state.shape[0]
    length_value = lineup_state.shape[1]
    residue_shard_count = pairwise.shape[0]
    alignment_heads_sharded = coupling_offset_weight_map.shape[1]
    pairwise_heads_sharded = triangle_bias_matrix.shape[1]
    inv_scale = 1.0 / math.sqrt(PER_FOCUS_DIM)
    row_place = lax.axis_index(("rows", "branch"))
    head_location = lax.axis_index("head")
    seq_start = row_place * sequence_shard_count
    row_start = row_place * residue_shard_count
    mask_full = span_mask(aligned_residue_bounds, length_value)
    mask_own = lax.dynamic_slice_in_dim(mask_full, seq_start, sequence_shard_count, 0)
    key_valid = residue_valid_mask > 0
    alignment_normed = layer_normalize(lineup_state).astype(jnp.bfloat16)
    pair_normed = layer_normalize(pairwise).astype(jnp.bfloat16)
    bias_matrix = jnp.concatenate([coupling_offset_weight_map, triangle_bias_matrix], axis=1)
    bias_local = jnp.einsum(
        "tue,el->ltu", pair_normed, bias_matrix, preferred_element_type=jnp.float32
    ).astype(jnp.bfloat16)
    lineup_mapped = jnp.einsum(
        "tvf,xfp->xtvp",
        alignment_normed,
        alignment_projection_matrix,
        preferred_element_type=jnp.float32,
    )
    lineup_probe_lookup_content = (
        lineup_mapped[:3]
        .astype(jnp.bfloat16)
        .reshape(3, sequence_shard_count, length_value, alignment_heads_sharded, PER_FOCUS_DIM)
    )
    alignment_gate = jax.nn.sigmoid(lineup_mapped[3])
    pair_proj = jnp.einsum(
        "ijc,gcd->gijd", pair_normed, pair_projection_matrix, preferred_element_type=jnp.float32
    )
    pair_qkv = (
        pair_proj[:3]
        .astype(jnp.bfloat16)
        .reshape(3, residue_shard_count, length_value, pairwise_heads_sharded, PER_FOCUS_DIM)
    )
    pair_gate = jax.nn.sigmoid(pair_proj[3])
    bias_portion = lax.all_gather(bias_local, ("rows", "branch"), axis=1, tiled=True)
    row_total_count = bias_portion.shape[1]
    alignment_query = lineup_probe_lookup_content[0]
    attention_scores = (
        jnp.einsum(
            "xtza,xfza->xztf",
            alignment_query,
            lineup_probe_lookup_content[1],
            preferred_element_type=jnp.float32,
        )
        * inv_scale
    )
    attention_scores = (
        attention_scores + bias_portion[:alignment_heads_sharded].astype(jnp.float32)[None]
    )
    attention_scores = jnp.where(mask_own[:, None, None, :] > 0, attention_scores, -1000000000.0)
    softmax_shares = soft_weights(attention_scores)
    alignment_portion = jnp.einsum(
        "fxkc,fcxz->fkxz",
        softmax_shares,
        lineup_probe_lookup_content[2],
        preferred_element_type=jnp.float32,
    )
    alignment_portion = alignment_portion.reshape(
        sequence_shard_count, row_total_count, alignment_heads_sharded * PER_FOCUS_DIM
    )
    alignment_portion = (alignment_portion * alignment_gate).astype(jnp.bfloat16)
    pair_query = pair_qkv[0]
    triangle_scores = (
        jnp.einsum("ijhd,ikhd->ihjk", pair_query, pair_qkv[1], preferred_element_type=jnp.float32)
        * inv_scale
    )
    triangle_scores = (
        triangle_scores + bias_portion[alignment_heads_sharded:].astype(jnp.float32)[None]
    )
    triangle_scores = jnp.where(key_valid[None, None, None, :], triangle_scores, -1000000000.0)
    tri_weights = soft_weights(triangle_scores)
    pair_part = jnp.einsum(
        "ihjk,ikhd->ijhd", tri_weights, pair_qkv[2], preferred_element_type=jnp.float32
    )
    pair_part = pair_part.reshape(
        residue_shard_count, row_total_count, pairwise_heads_sharded * PER_FOCUS_DIM
    )
    pair_part = (pair_part * pair_gate).astype(jnp.bfloat16)
    alignment_flattened = jnp.transpose(alignment_portion, (1, 0, 2)).reshape(
        row_total_count, sequence_shard_count * alignment_heads_sharded * PER_FOCUS_DIM
    )
    pair_flattened = jnp.transpose(pair_part, (1, 0, 2)).reshape(
        row_total_count, residue_shard_count * pairwise_heads_sharded * PER_FOCUS_DIM
    )
    attention_result = jnp.concatenate([alignment_flattened, pair_flattened], axis=1)
    alignment_width = sequence_shard_count * alignment_heads_sharded * PER_FOCUS_DIM
    alignment_local = jnp.transpose(
        attention_result[:, :alignment_width].reshape(
            length_value, sequence_shard_count, alignment_heads_sharded * PER_FOCUS_DIM
        ),
        (1, 0, 2),
    )
    pair_local = jnp.transpose(
        attention_result[:, alignment_width:].reshape(
            length_value, residue_shard_count, pairwise_heads_sharded * PER_FOCUS_DIM
        ),
        (1, 0, 2),
    )
    lineup_focus_split, pairwise_heads = (
        lax.all_gather(alignment_local, "head", axis=2, tiled=True),
        lax.all_gather(pair_local, "head", axis=2, tiled=True),
    )
    outer_factors = jnp.einsum(
        "juf,bfn->bjun", alignment_normed, left_right_maps, preferred_element_type=jnp.float32
    )
    outer_factors = (outer_factors * mask_own[None, :, :, None]).astype(jnp.bfloat16)
    factor_rows = lax.all_to_all(
        outer_factors[0], ("rows", "branch"), split_axis=1, concat_axis=0, tiled=True
    )
    col_factors = lax.all_gather(outer_factors[1], ("rows", "branch"), axis=0, tiled=True)
    mask_rows = lax.dynamic_slice_in_dim(mask_full, row_start, residue_shard_count, 1)
    pair_count = jnp.dot(mask_rows.T, mask_full, precision=lax.Precision.HIGHEST)
    col_block = math.gcd(length_value, 128)

    def outer_block(col_start):
        block_cols = lax.dynamic_slice_in_dim(col_factors, col_start, col_block, 1)
        outer_sum = lax.dot_general(
            factor_rows, block_cols, (((0,), (0,)), ((), ())), preferred_element_type=jnp.float32
        )
        counts = lax.dynamic_slice_in_dim(pair_count, col_start, col_block, 1)
        outer_mean = (outer_sum / counts[:, None, :, None]).astype(jnp.bfloat16)
        outer_mean = jnp.transpose(outer_mean, (0, 2, 1, 3)).reshape(
            residue_shard_count * col_block, -1
        )
        return jnp.dot(
            outer_mean, outer_product_output_matrix, preferred_element_type=jnp.float32
        ).reshape(residue_shard_count, col_block, -1)

    starts = jnp.arange(length_value // col_block, dtype=jnp.int32) * col_block
    opm_blocks = lax.map(outer_block, starts)
    opm_update = jnp.transpose(opm_blocks, (1, 0, 2, 3)).reshape(
        residue_shard_count, length_value, -1
    )
    width_z = pair_output_matrix.shape[1]
    tri_update = jnp.dot(
        pairwise_heads.reshape(residue_shard_count * length_value, -1),
        pair_output_matrix,
        preferred_element_type=jnp.float32,
    ).reshape(residue_shard_count, length_value, width_z)
    pair_own = lax.dynamic_slice_in_dim(pairwise, head_location * width_z, width_z, 2).astype(
        jnp.float32
    )
    pairwise_out = (pair_own + tri_update + opm_update).astype(jnp.bfloat16)
    channels = lineup_state.shape[2]
    lineup_blended = lineup_state.astype(jnp.float32) + jnp.dot(
        lineup_focus_split.reshape(sequence_shard_count * length_value, -1),
        lineup_readout_weight,
        preferred_element_type=jnp.float32,
    ).reshape(sequence_shard_count, length_value, channels)
    feedfwd_standardized = layer_normalize(lineup_blended).astype(jnp.bfloat16)
    head_count = lax.axis_size("head")
    hidden = jax.nn.relu(
        jnp.einsum(
            "src,cf->srf",
            feedfwd_standardized,
            feedfwd_entry_weight,
            preferred_element_type=jnp.float32,
        )
    ).astype(jnp.bfloat16)
    partial_value = jnp.einsum(
        "srf,fc->src", hidden, feedfwd_exit_weight, preferred_element_type=jnp.float32
    )
    summed_result = lax.psum_scatter(
        partial_value.astype(jnp.bfloat16), "head", scatter_dimension=2, tiled=True
    ).astype(jnp.float32)
    alignment_channel_width = channels // head_count
    alignment_owned = lax.dynamic_slice_in_dim(
        lineup_blended, head_location * alignment_channel_width, alignment_channel_width, 2
    )
    refreshed_lineup_state = (alignment_owned + summed_result).astype(jnp.bfloat16)
    return (refreshed_lineup_state, pairwise_out)


def solution(mesh):
    in_specs = (
        P(("parts", "rows", "branch"), None, None),
        P(("parts", "rows", "branch"), None, None),
        P("parts", None),
        P("parts"),
        P(None, "head"),
        P(None, "head"),
        P(None, None, "head"),
        P(),
        P(None, "head"),
        P("head", None),
        P(None, None, "head"),
        P(None, "head"),
        P(),
        P(None, "head"),
    )
    out_specs = (
        P(("parts", "rows", "branch"), None, "head"),
        P(("parts", "rows", "branch"), None, "head"),
    )
    return jax.shard_map(local, mesh=mesh, in_specs=in_specs, out_specs=out_specs, check_vma=False)
```

profile of v0, /device:TPU:0, one launch (start us, length us, event | category | flops | bytes accessed | tf_op | source)
XLA Modules:
  0.0 93.5 jit_solution(9554350493809274063)
XLA Ops:
  7.2 0.0 copy-start
  7.2 0.0 copy-start.2
  7.2 1.1 %convert_reduce_fusion.1 = f32[2,128]{1,0:T(2,128)S(1)} fusion(bf16[2,128,256]{2,1,0:T(8,128)(2,1)} %param.14), kind=kLoop, calls=%fused_computation.38 | loop fusion | flops 130816 | bytes 132096 | tf_op jit(solution)/shard_map/reduce_sum | solution.py:12
  8.3 1.1 %fusion.24 = f32[2,128]{1,0:T(2,128)S(1)} fusion(bf16[2,128,256]{2,1,0:T(8,128)(2,1)} %param.14, f32[2,128]{1,0:T(2,128)S(1)} %broadcast_multiply_fusion.2), kind=kLoop, calls=%fused_computation.41 | loop fusion | flops 261888 | bytes 133120 | tf_op jit(solution)/shard_map/reduce_sum | solution.py:13
  9.4 0.8 slice_bitcast_fusion.2
  10.1 0.1 fusion.62
  10.2 1.2 %fusion.16 = bf16[2,2,128,32]{2,3,0,1:T(8,128)(2,1)S(1)} fusion(bf16[2,128,256]{2,1,0:T(8,128)(2,1)} %param.14, f32[2,128]{1,0:T(2,128)S(1)} %add_rsqrt_fusion.2, f32[2,128]{1,0:T(2,128)S(1)} %broadcast_multiply_fusion.2, bf16[2,256,32]{1,2,0:T(8,128)(2,1)} %param.26, f32[2,128]{1,0:T(2,128)S(1)} %get-tuple-element.28), kind=kOutput, calls=%fused_computation.26 | convolution fusion | flops 8683520 | bytes 199680 | tf_op jit(solution)/shard_map/juf,bfn->bjun/dot_general | solution.py:155
  11.4 0.1 copy.46
  11.6 0.7 reshape.117
  12.3 7.4 %all-to-all-start = ((bf16[16,2,256]{2,1,0:T(2,128)(2,1)}), bf16[16,2,256]{2,1,0:T(2,128)(2,1)S(1)}, u32[]{:S(2)}, u32[]{:S(2)}) async-start(bf16[16,2,256]{2,1,0:T(2,128)(2,1)} %reshape.117), calls=%async_computation | async-start | bytes 32768 | tf_op jit(solution)/shard_map/all_to_all | solution.py:159
  19.7 0.0 reduce-scatter.4.cloned.1.call-start
  19.7 1.1 %convert_reduce_fusion = f32[8,128]{1,0:T(8,128)S(1)} fusion(bf16[8,128,128]{2,1,0:T(8,128)(2,1)} %param.15), kind=kLoop, calls=%fused_computation.30 | loop fusion | flops 261120 | bytes 266240 | tf_op jit(solution)/shard_map/reduce_sum | solution.py:12
  20.9 1.3 %fusion.19 = f32[8,128]{1,0:T(8,128)S(1)} fusion(bf16[8,128,128]{2,1,0:T(8,128)(2,1)} %param.15, f32[8,128]{1,0:T(8,128)S(1)} %broadcast_multiply_fusion), kind=kLoop, calls=%fused_computation.33 | loop fusion | flops 523264 | bytes 270336 | tf_op jit(solution)/shard_map/reduce_sum | solution.py:13
  22.2 1.4 %convolution_convert_fusion = bf16[6,8,128]{2,0,1:T(8,128)(2,1)S(1)} fusion(bf16[8,128,128]{2,1,0:T(8,128)(2,1)} %param.15, f32[8,128]{1,0:T(8,128)S(1)} %add_rsqrt_fusion, f32[8,128]{1,0:T(8,128)S(1)} %broadcast_multiply_fusion, bf16[128,2]{0,1:T(2,128)(2,1)} %param.19, bf16[128,4]{0,1:T(4,128)(2,1)} %param.18), kind=kOutput, calls=%fused_computation.27 | convolution fusion | flops 2106368 | bytes 284160 | tf_op jit(solution)/shard_map/tue,el->ltu/dot_general | solution.py:63
  23.6 22.2 %all_gather.12 = bf16[6,128,128]{2,1,0:T(8,128)(2,1)S(1)} all-gather(bf16[6,8,128]{2,1,0:T(8,128)(2,1)S(1)} %copy.39), channel_id=1, replica_groups=mesh['parts'=1,'rows'=8,'branch'=2,'head'=2] {'rows','branch'}, dimensions={1}, use_global_device_ids=true | all-gather | bytes 208896 | tf_op jit(solution)/shard_map/all_gather | solution.py:87
  45.9 0.1 copy.40
  46.1 0.4 fusion.78
  46.5 0.4 fusion.79
  46.9 0.0 copy-start.8
  46.9 0.3 fusion.10
  47.2 0.2 fusion.40
  47.5 5.1 %all_gather.13 = bf16[2,128,256]{1,2,0:T(8,128)(2,1)S(1)} all-gather(bf16[2,128,128]{1,2,0:T(8,128)(2,1)S(1)} %fusion.55), channel_id=1, replica_groups=mesh['parts'=1,'rows'=8,'branch'=2,'head'=2] {'head'}, dimensions={2}, use_global_device_ids=true | all-gather | bytes 196608 | tf_op jit(solution)/shard_map/all_gather | solution.py:152
  52.6 0.3 fusion.80
  53.0 0.2 multiply_reduce_fusion
  53.2 0.4 fusion.14
  53.6 0.1 copy.64
  53.7 0.7 copy.76
  54.4 0.0 reduce-scatter.4.cloned.1.call-update
  54.5 0.1 copy.44
  54.6 0.9 fusion.81
  55.5 0.6 fusion.82
  56.1 0.4 fusion.6
  56.4 0.3 fusion.63
  56.7 0.1 constant_dynamic-slice_fusion
  56.9 0.1 copy.66
  57.0 0.3 fusion.21
  57.4 0.1 fusion.39
  57.4 6.6 %all_gather.14 = bf16[8,128,128]{1,2,0:T(8,128)(2,1)S(1)} all-gather(bf16[8,128,64]{1,2,0:T(8,128)(2,1)S(1)} %fusion.39), channel_id=1, replica_groups=mesh['parts'=1,'rows'=8,'branch'=2,'head'=2] {'head'}, dimensions={2}, use_global_device_ids=true | all-gather | bytes 393216 | tf_op jit(solution)/shard_map/all_gather | solution.py:153
  64.0 0.2 convolution_add_fusion.1
  64.2 17.8 %all-gather = bf16[1,32,128,32]{2,3,0,1:T(8,128)(2,1)S(1)} all-gather(bf16[1,2,128,32]{2,3,0,1:T(8,128)(2,1)S(1)} %get-tuple-element.27), channel_id=2, replica_groups=mesh['parts'=1,'rows'=8,'branch'=2,'head'=2] {'rows','branch'}, dimensions={1}, use_global_device_ids=true | all-gather | bytes 278528 | tf_op jit(solution)/shard_map/all_gather | solution.py:162
  82.1 0.1 reshape.118
  82.2 0.7 fusion.2
  83.0 0.8 copy.51
  83.8 0.1 copy-done.4
  83.9 1.1 %fusion.13 = bf16[8,128,64]{1,2,0:T(8,128)(2,1)} fusion(f32[8,128,64]{1,2,0:T(8,128)S(1)} %convolution_add_fusion.1, bf16[8,128,1024]{1,2,0:T(8,128)(2,1)S(1)} %bitcast.130, bf16[1024,64]{0,1:T(8,128)(2,1)S(1)} %copy-done.4), kind=kOutput, calls=%fused_computation.22 | convolution fusion | flops 134348800 | bytes 2621440 | tf_op jit(solution)/shard_map/while/body/eval_jaxpr/dot_general | solution.py:177
  85.0 0.9 reshape.116
  85.9 0.1 copy.65
  86.0 0.7 add_convert_fusion
  (35 shorter events, 0.3 us)
Async XLA Ops:
  7.2 38.9 %copy-start = (bf16[4,256,128]{2,1,0:T(8,128)(2,1)S(1)}, bf16[4,256,128]{2,1,0:T(8,128)(2,1)}, u32[]{:S(2)}) copy-start(bf16[4,256,128]{2,1,0:T(8,128)(2,1)} %param.20) | copy-start | bytes 786436
  7.2 38.9 %copy-start.2 = (bf16[2,128,256]{2,1,0:T(8,128)(2,1)S(1)}, bf16[2,128,256]{2,1,0:T(8,128)(2,1)}, u32[]{:S(2)}) copy-start(bf16[2,128,256]{2,1,0:T(8,128)(2,1)} %param.14) | copy-start | bytes 393220
  12.3 69.8 %all-to-all-start = ((bf16[16,2,256]{2,1,0:T(2,128)(2,1)}), bf16[16,2,256]{2,1,0:T(2,128)(2,1)S(1)}, u32[]{:S(2)}, u32[]{:S(2)}) async-start(bf16[16,2,256]{2,1,0:T(2,128)(2,1)} %reshape.117), calls=%async_computation | async-start | bytes 32768 | tf_op jit(solution)/shard_map/all_to_all | solution.py:159
  19.7 65.3 %reduce-scatter.4.cloned.1.call-start = ((), (), s32[]{:S(2)}) async-start(), calls=%async_computation.2 | async-start | bytes 196608
  46.8 5.8 %copy-start.3 = (bf16[256,256]{1,0:T(8,128)(2,1)S(1)}, bf16[256,256]{1,0:T(8,128)(2,1)}, u32[]{:S(2)}) copy-start(bf16[256,256]{1,0:T(8,128)(2,1)} %param.21) | copy-start | bytes 393220
  46.9 6.3 %copy-start.7 = (bf16[512,256]{1,0:T(8,128)(2,1)S(1)}, bf16[512,256]{1,0:T(8,128)(2,1)}, u32[]{:S(2)}) copy-start(bf16[512,256]{1,0:T(8,128)(2,1)} %param.23) | copy-start | bytes 786436
  46.9 6.3 %copy-start.8 = (bf16[256,512]{1,0:T(8,128)(2,1)S(1)}, bf16[256,512]{1,0:T(8,128)(2,1)}, u32[]{:S(2)}) copy-start(bf16[256,512]{1,0:T(8,128)(2,1)} %param.22) | copy-start | bytes 786436
  47.4 7.0 %copy-start.9 = (s32[128]{0:T(128)S(1)}, s32[128]{0:T(128)}, u32[]{:S(2)}) copy-start(s32[128]{0:T(128)} %param.17) | copy-start | bytes 1540
  47.4 7.2 %copy-start.1 = (bf16[8,128,128]{2,1,0:T(8,128)(2,1)S(1)}, bf16[8,128,128]{2,1,0:T(8,128)(2,1)}, u32[]{:S(2)}) copy-start(bf16[8,128,128]{2,1,0:T(8,128)(2,1)} %param.15) | copy-start | bytes 786436
  47.4 7.2 %copy-start.5 = (bf16[4,128,64]{1,2,0:T(8,128)(2,1)S(1)}, bf16[4,128,64]{1,2,0:T(8,128)(2,1)}, u32[]{:S(2)}) copy-start(bf16[4,128,64]{1,2,0:T(8,128)(2,1)} %param.24) | copy-start | bytes 196612
  57.0 7.0 %copy-start.6 = (bf16[128,64]{0,1:T(8,128)(2,1)S(1)}, bf16[128,64]{0,1:T(8,128)(2,1)}, u32[]{:S(2)}) copy-start(bf16[128,64]{0,1:T(8,128)(2,1)} %param.25) | copy-start | bytes 49156
  82.9 0.9 copy-start.4
Sparse Core Ops, SparseCore 0:
  54.5 8.4 reduce-scatter.3
where the time goes:
time: 93.9 us; the launch traced here: 93.5 us
  blocking collectives  51.8 us (55%)
  between operations  14.4 us (15%)
  matrix products  9.08 us (10%)
  starting transfers between devices  7.45 us (8%)
  other arithmetic  5.69 us (6%)
  local copies, waits for them, and re-layouts  4.99 us (5%)
    all_gather x1, blocking collectives, local(): lax.all_gather(bias_local, ('rows', 'branch'), axis=1, tiled=True)  22.2 us
    all_gather x1, blocking collectives, local(): lax.all_gather(outer_factors[1], ('rows', 'branch'), axis=0, tiled=True)  17.8 us
    all_to_all x1, starting transfers between devices, local(): lax.all_to_all(outer_factors[0], ('rows', 'branch'), split_axis=1, concat...  7.41 us
    all_gather x1, blocking collectives, local(): lax.all_gather(pair_local, 'head', axis=2, tiled=True)  6.59 us
    all_gather x1, blocking collectives, local(): lax.all_gather(alignment_local, 'head', axis=2, tiled=True)  5.14 us
    unnamed x27, local copies, waits for them, and re-layouts  2.84 us
    reduce_sum x3, other arithmetic, layer_normalize(): spread = jnp.mean(center * center, -1, keepdims=True)  2.59 us
    reduce_sum x2, other arithmetic, layer_normalize(): center = values - jnp.mean(values, -1, keepdims=True)  2.16 us
  transfers between devices with their start and end apart: 2, of which 0 were waited for; matrix products, arithmetic and copies ran while one was open for 14% of the time, Pallas kernels for 0%

commit v1 on v0

--- a/solution.py
+++ b/solution.py
@@ -156,9 +156,10 @@
         "juf,bfn->bjun", alignment_normed, left_right_maps, preferred_element_type=jnp.float32
     )
     outer_factors = (outer_factors * mask_own[None, :, :, None]).astype(jnp.bfloat16)
-    factor_rows = lax.all_to_all(
-        outer_factors[0], ("rows", "branch"), split_axis=1, concat_axis=0, tiled=True
-    )
+    block = outer_factors[0]
+    parts = jnp.split(block, lax.axis_size(("rows", "branch")), axis=1)
+    arrived = lax.all_to_all(jnp.stack(parts), ("rows", "branch"), 0, 0)
+    factor_rows = jnp.concatenate(arrived, axis=0)
     col_factors = lax.all_gather(outer_factors[1], ("rows", "branch"), axis=0, tiled=True)
     mask_rows = lax.dynamic_slice_in_dim(mask_full, row_start, residue_shard_count, 1)
     pair_count = jnp.dot(mask_rows.T, mask_full, precision=lax.Precision.HIGHEST)

time: 93.9 us -> 93.3 us (level)
  local copies, waits for them, and re-layouts: 4.99 us -> 6.46 us
  matrix products: 9.08 us -> 8.1 us
  other arithmetic: 5.69 us -> 4.73 us
    another operation x0 -> x18, local copies, waits for them, and re-layouts: none -> 1.48 us  [local(): arrived = lax.all_to_all(jnp.stack(parts), ('rows', 'branch'), 0, 0)]
    dot_general x1, matrix products: 1.43 us -> 0.45 us  [local(): jnp.einsum('tue,el->ltu', pair_normed, bias_matrix, preferred_element_typ...]
    reduce_sum x3, other arithmetic: 2.59 us -> 1.63 us  [layer_normalize(): spread = jnp.mean(center * center, -1, keepdims=True)]
    unnamed x27 -> x46, local copies, waits for them, and re-layouts: 2.84 us -> 2.97 us
  transfers between devices with their start and end apart: 2 -> 2, of which waited for: 0 -> 0; matrix products, arithmetic and copies ran while one was open for 14% -> 12% of each run, Pallas kernels for 0% -> 0%
where the time goes in v1:
time: 93.3 us; the launch traced here: 92.9 us
  blocking collectives  51.7 us (55%)
  between operations  14.5 us (16%)
  matrix products  8.1 us (9%)
  starting transfers between devices  7.45 us (8%)
  local copies, waits for them, and re-layouts  6.46 us (7%)
  other arithmetic  4.73 us (5%)
    all_gather x1, blocking collectives, local(): lax.all_gather(bias_local, ('rows', 'branch'), axis=1, tiled=True)  22.2 us
    all_gather x1, blocking collectives, local(): lax.all_gather(outer_factors[1], ('rows', 'branch'), axis=0, tiled=True)  17.8 us
    all_to_all x1, starting transfers between devices, local(): arrived = lax.all_to_all(jnp.stack(parts), ('rows', 'branch'), 0, 0)  7.41 us
    all_gather x1, blocking collectives, local(): lax.all_gather(pair_local, 'head', axis=2, tiled=True)  6.59 us
    all_gather x1, blocking collectives, local(): lax.all_gather(alignment_local, 'head', axis=2, tiled=True)  5.01 us
    unnamed x46, local copies, waits for them, and re-layouts  2.97 us
    reduce_sum x2, other arithmetic, layer_normalize(): center = values - jnp.mean(values, -1, keepdims=True)  2.16 us
  transfers between devices with their start and end apart: 2, of which 0 were waited for; matrix products, arithmetic and copies ran while one was open for 12% of the time, Pallas kernels for 0%

profile of v1, /device:TPU:0, one launch (start us, length us, event | category | flops | bytes accessed | tf_op | source)
XLA Modules:
  0.0 92.9 jit_solution(5612878842681667742)
XLA Ops:
  7.2 1.1 %convert_reduce_fusion.1 = f32[2,128]{1,0:T(2,128)S(1)} fusion(bf16[2,128,256]{2,1,0:T(8,128)(2,1)} %param.14), kind=kLoop, calls=%fused_computation.38 | loop fusion | flops 130816 | bytes 132096 | tf_op jit(solution)/shard_map/reduce_sum | solution.py:12
  8.3 1.1 %fusion.24 = f32[2,128]{1,0:T(2,128)S(1)} fusion(bf16[2,128,256]{2,1,0:T(8,128)(2,1)} %param.14, f32[2,128]{1,0:T(2,128)S(1)} %broadcast_multiply_fusion.2), kind=kLoop, calls=%fused_computation.41 | loop fusion | flops 261888 | bytes 133120 | tf_op jit(solution)/shard_map/reduce_sum | solution.py:13
  9.4 0.8 slice_bitcast_fusion.18
  10.3 1.2 %fusion.16 = bf16[2,2,128,32]{2,3,0,1:T(8,128)(2,1)S(1)} fusion(bf16[2,128,256]{2,1,0:T(8,128)(2,1)} %param.14, f32[2,128]{1,0:T(2,128)S(1)} %add_rsqrt_fusion.2, f32[2,128]{1,0:T(2,128)S(1)} %broadcast_multiply_fusion.2, bf16[2,256,32]{1,2,0:T(8,128)(2,1)} %param.26, f32[2,128]{1,0:T(2,128)S(1)} %get-tuple-element.44), kind=kOutput, calls=%fused_computation.26 | convolution fusion | flops 8683520 | bytes 199680 | tf_op jit(solution)/shard_map/juf,bfn->bjun/dot_general | solution.py:155
  11.5 0.1 slice_bitcast_fusion
  11.9 0.1 copy.83
  12.0 0.1 copy.82
  12.1 0.1 copy.81
  12.3 0.1 copy.79
  12.4 0.1 copy.78
  12.4 0.1 copy.77
  12.5 0.1 copy.76
  12.6 0.1 copy.75
  13.1 0.7 reshape.121
  13.9 7.4 %all-to-all-start = ((bf16[16,2,256]{2,1,0:T(2,128)(2,1)}), bf16[16,2,256]{2,1,0:T(2,128)(2,1)S(1)}, u32[]{:S(2)}, u32[]{:S(2)}) async-start(bf16[16,2,256]{2,1,0:T(2,128)(2,1)} %reshape.121), calls=%async_computation | async-start | bytes 32768 | tf_op jit(solution)/shard_map/all_to_all | solution.py:161
  21.3 1.1 %convert_reduce_fusion = f32[8,128]{1,0:T(8,128)S(1)} fusion(bf16[8,128,128]{2,1,0:T(8,128)(2,1)} %param.15), kind=kLoop, calls=%fused_computation.30 | loop fusion | flops 261120 | bytes 266240 | tf_op jit(solution)/shard_map/reduce_sum | solution.py:12
  22.4 0.4 fusion.19
  22.8 0.5 convolution_convert_fusion
  23.3 22.2 %all_gather.12 = bf16[6,128,128]{2,1,0:T(8,128)(2,1)S(1)} all-gather(bf16[6,8,128]{2,1,0:T(8,128)(2,1)S(1)} %copy.65), channel_id=1, replica_groups=mesh['parts'=1,'rows'=8,'branch'=2,'head'=2] {'rows','branch'}, dimensions={1}, use_global_device_ids=true | all-gather | bytes 208896 | tf_op jit(solution)/shard_map/all_gather | solution.py:87
  45.6 0.1 copy.66
  45.7 0.4 fusion.78
  46.1 0.4 fusion.79
  46.5 0.3 fusion.10
  46.8 0.2 fusion.40
  47.1 5.0 %all_gather.13 = bf16[2,128,256]{1,2,0:T(8,128)(2,1)S(1)} all-gather(bf16[2,128,128]{1,2,0:T(8,128)(2,1)S(1)} %fusion.55), channel_id=1, replica_groups=mesh['parts'=1,'rows'=8,'branch'=2,'head'=2] {'head'}, dimensions={2}, use_global_device_ids=true | all-gather | bytes 196608 | tf_op jit(solution)/shard_map/all_gather | solution.py:152
  52.1 0.3 fusion.80
  52.5 0.2 multiply_reduce_fusion
  52.7 0.4 fusion.14
  53.1 0.1 copy.103
  53.2 0.7 copy.114
  54.0 0.1 copy.70
  54.1 0.9 fusion.81
  55.0 0.6 fusion.82
  55.6 0.4 fusion.6
  55.9 0.3 fusion.63
  56.2 0.1 constant_dynamic-slice_fusion
  56.3 0.1 copy.105
  56.5 0.3 fusion.21
  56.9 6.6 %all_gather.14 = bf16[8,128,128]{1,2,0:T(8,128)(2,1)S(1)} all-gather(bf16[8,128,64]{1,2,0:T(8,128)(2,1)S(1)} %fusion.39), channel_id=1, replica_groups=mesh['parts'=1,'rows'=8,'branch'=2,'head'=2] {'head'}, dimensions={2}, use_global_device_ids=true | all-gather | bytes 393216 | tf_op jit(solution)/shard_map/all_gather | solution.py:153
  63.5 0.2 convolution_add_fusion.1
  63.7 17.8 %all-gather = bf16[1,32,128,32]{2,3,0,1:T(8,128)(2,1)S(1)} all-gather(bf16[1,2,128,32]{2,3,0,1:T(8,128)(2,1)S(1)} %get-tuple-element.27), channel_id=2, replica_groups=mesh['parts'=1,'rows'=8,'branch'=2,'head'=2] {'rows','branch'}, dimensions={1}, use_global_device_ids=true | all-gather | bytes 278528 | tf_op jit(solution)/shard_map/all_gather | solution.py:163
  81.6 0.1 reshape.122
  81.7 0.7 fusion.2
  82.4 0.8 copy.90
  83.3 1.1 %fusion.13 = bf16[8,128,64]{1,2,0:T(8,128)(2,1)} fusion(f32[8,128,64]{1,2,0:T(8,128)S(1)} %convolution_add_fusion.1, bf16[8,128,1024]{1,2,0:T(8,128)(2,1)S(1)} %bitcast.155, bf16[1024,64]{0,1:T(8,128)(2,1)S(1)} %copy-done.4), kind=kOutput, calls=%fused_computation.22 | convolution fusion | flops 134348800 | bytes 2621440 | tf_op jit(solution)/shard_map/while/body/eval_jaxpr/dot_general | solution.py:178
  84.4 0.9 reshape.120
  85.3 0.1 copy.104
  85.4 0.7 add_convert_fusion
  (69 shorter events, 1.3 us)
Async XLA Ops:
  7.2 38.5 %copy-start = (bf16[4,256,128]{2,1,0:T(8,128)(2,1)S(1)}, bf16[4,256,128]{2,1,0:T(8,128)(2,1)}, u32[]{:S(2)}) copy-start(bf16[4,256,128]{2,1,0:T(8,128)(2,1)} %param.20) | copy-start | bytes 786436
  7.2 38.5 %copy-start.2 = (bf16[2,128,256]{2,1,0:T(8,128)(2,1)S(1)}, bf16[2,128,256]{2,1,0:T(8,128)(2,1)}, u32[]{:S(2)}) copy-start(bf16[2,128,256]{2,1,0:T(8,128)(2,1)} %param.14) | copy-start | bytes 393220
  7.2 15.2 %copy-start.1 = (bf16[8,128,128]{2,1,0:T(8,128)(2,1)S(1)}, bf16[8,128,128]{2,1,0:T(8,128)(2,1)}, u32[]{:S(2)}) copy-start(bf16[8,128,128]{2,1,0:T(8,128)(2,1)} %param.15) | copy-start | bytes 786436
  7.2 15.6 %copy-start.10 = (bf16[128,2]{0,1:T(2,128)(2,1)S(1)}, bf16[128,2]{0,1:T(2,128)(2,1)}, u32[]{:S(2)}) copy-start(bf16[128,2]{0,1:T(2,128)(2,1)} %param.19) | copy-start | bytes 1540
  7.2 15.6 %copy-start.9 = (bf16[128,4]{0,1:T(4,128)(2,1)S(1)}, bf16[128,4]{0,1:T(4,128)(2,1)}, u32[]{:S(2)}) copy-start(bf16[128,4]{0,1:T(4,128)(2,1)} %param.18) | copy-start | bytes 3076
  13.9 67.7 %all-to-all-start = ((bf16[16,2,256]{2,1,0:T(2,128)(2,1)}), bf16[16,2,256]{2,1,0:T(2,128)(2,1)S(1)}, u32[]{:S(2)}, u32[]{:S(2)}) async-start(bf16[16,2,256]{2,1,0:T(2,128)(2,1)} %reshape.121), calls=%async_computation | async-start | bytes 32768 | tf_op jit(solution)/shard_map/all_to_all | solution.py:161
  21.3 63.2 %reduce-scatter.4.cloned.1.call-start = ((), (), s32[]{:S(2)}) async-start(), calls=%async_computation.2 | async-start | bytes 196608
  46.5 5.6 %copy-start.3 = (bf16[256,256]{1,0:T(8,128)(2,1)S(1)}, bf16[256,256]{1,0:T(8,128)(2,1)}, u32[]{:S(2)}) copy-start(bf16[256,256]{1,0:T(8,128)(2,1)} %param.21) | copy-start | bytes 393220
  46.5 6.1 %copy-start.7 = (bf16[512,256]{1,0:T(8,128)(2,1)S(1)}, bf16[512,256]{1,0:T(8,128)(2,1)}, u32[]{:S(2)}) copy-start(bf16[512,256]{1,0:T(8,128)(2,1)} %param.23) | copy-start | bytes 786436
  46.5 6.1 %copy-start.8 = (bf16[256,512]{1,0:T(8,128)(2,1)S(1)}, bf16[256,512]{1,0:T(8,128)(2,1)}, u32[]{:S(2)}) copy-start(bf16[256,512]{1,0:T(8,128)(2,1)} %param.22) | copy-start | bytes 786436
  47.1 6.9 %copy-start.11 = (s32[128]{0:T(128)S(1)}, s32[128]{0:T(128)}, u32[]{:S(2)}) copy-start(s32[128]{0:T(128)} %param.17) | copy-start | bytes 1540
  47.1 7.0 %copy-start.5 = (bf16[4,128,64]{1,2,0:T(8,128)(2,1)S(1)}, bf16[4,128,64]{1,2,0:T(8,128)(2,1)}, u32[]{:S(2)}) copy-start(bf16[4,128,64]{1,2,0:T(8,128)(2,1)} %param.24) | copy-start | bytes 196612
  56.5 7.0 %copy-start.6 = (bf16[128,64]{0,1:T(8,128)(2,1)S(1)}, bf16[128,64]{0,1:T(8,128)(2,1)}, u32[]{:S(2)}) copy-start(bf16[128,64]{0,1:T(8,128)(2,1)} %param.25) | copy-start | bytes 49156
  82.4 0.9 copy-start.4
Sparse Core Ops, SparseCore 0:
  54.0 8.4 reduce-scatter.3
